TPU v7x, 768 devices: a whole 4x8x12 slice. The times are simulated.
768 devices in a mesh: pipe: 4 (over y_hi), win: 48 (over z, y_lo, core), head: 4 (over x).
Axes of the slice: x: 4, y: 8 (y_hi: 4, y_lo: 2; y = y_hi * 2 + y_lo), z: 12, core: 2. Of those that a mesh axis runs over, the one named last changes fastest.
Arguments:
- stream: bfloat16 [8, 1536, 2048], P('head', 'win'), may hold values from -16 to 16
- score_scale: float32 [4, 2048], P('pipe'), may hold values from -12 to 12
- value_weight: bfloat16 [4, 2048, 2048], P('pipe', None, 'head'), may hold values from -0.125 to 0.125
- out_weight: bfloat16 [4, 2048, 2048], P('pipe', 'head'), may hold values from -0.25 to 0.25
Outputs:
- sections: bfloat16 [4, 8, 1536, 2048], P('pipe', None, 'win', 'head')
All inputs are finite; a program needn't handle non-finite values.
Results may differ from a plain program's by a relative error of at most 0.03.
Values may be sent and summed in bfloat16 or wider, within the bound.
A program may use at most 32 MiB of HBM per device.

v0:
```python
import math

import jax
import jax.numpy as jnp
from jax import lax
from jax.sharding import PartitionSpec as P

HEAD_DIM = 128
WIN = 32


EPSILON = 1e-06


def from_behind(value, axis, steps):
    count = lax.axis_size(axis)
    pairs = [(source, (source + steps) % count) for source in range(count)]
    return lax.ppermute(value, axis, pairs)


def from_behind_2(value, axis, steps):
    count = lax.axis_size(axis)
    leading, last = (max(0, -steps), min(count, count - steps))
    return lax.ppermute(value, axis, [(source, source + steps) for source in range(leading, last)])


def to_windows(tensor, window_count, heads_local):
    row_count = tensor.shape[0]
    shaped = tensor.reshape(row_count, window_count, WIN, heads_local, HEAD_DIM)
    shaped = shaped.transpose(1, 3, 0, 2, 4)
    return shaped.reshape(window_count * heads_local, row_count * WIN, HEAD_DIM)


def attend(framed, complete, query_scale, value_cols):
    row_count, col_count, channels = framed.shape
    heads_local = channels // HEAD_DIM
    window_count = col_count // WIN
    inv_root = 1.0 / math.sqrt(HEAD_DIM)
    queries = (framed.astype(jnp.float32) * query_scale).astype(jnp.bfloat16)
    values = jnp.dot(
        complete.reshape(row_count * col_count, complete.shape[2]),
        value_cols,
        preferred_element_type=jnp.float32,
    )
    values = values.astype(jnp.bfloat16).reshape(row_count, col_count, channels)
    windowed_queries = to_windows(queries, window_count, heads_local)
    windowed_keys = to_windows(framed, window_count, heads_local)
    windowed_values = to_windows(values, window_count, heads_local)
    scores = (
        jnp.einsum(
            "foa,fxa->fox", windowed_queries, windowed_keys, preferred_element_type=jnp.float32
        )
        * inv_root
    )
    score_maximum = jnp.max(scores, axis=2, keepdims=True)
    exp_scores = jnp.exp(scores - score_maximum)
    attention_probabilities = (exp_scores / jnp.sum(exp_scores, axis=2, keepdims=True)).astype(
        jnp.bfloat16
    )
    attended = jnp.einsum(
        "eom,eml->eol", attention_probabilities, windowed_values, preferred_element_type=jnp.float32
    ).astype(jnp.bfloat16)
    attended = attended.reshape(window_count, heads_local, row_count, WIN, HEAD_DIM)
    return attended.transpose(2, 0, 3, 1, 4).reshape(row_count, col_count, channels)


def per_device(stream, score_scale, value_weight, out_weight):
    gathered = lax.all_to_all(stream, "head", split_axis=2, concat_axis=0, tiled=True)
    row_count, col_count, channels = gathered.shape
    half_win = WIN // 2
    segment_id = lax.axis_index("pipe")
    sections = lax.axis_size("pipe")
    width_all = channels * lax.axis_size("head")
    first_chan = lax.axis_index("head") * channels
    query_scale = lax.dynamic_slice_in_dim(score_scale[0], first_chan, channels, 0)
    value_cols = value_weight[0]
    out_rows = out_weight[0]
    current = gathered
    recorded = jnp.zeros_like(gathered)
    for section in range(sections):
        active = segment_id == section
        shifted = section % 2 == 1
        current_f = current.astype(jnp.float32)
        partial_value = jnp.sum(current_f * current_f, axis=2)
        square_sums = lax.psum(partial_value, "head")
        inverse = lax.rsqrt(square_sums / width_all + EPSILON)
        normed = (current_f * inverse[:, :, None]).astype(jnp.bfloat16)
        framed = normed
        if shifted:
            next_section = from_behind(normed[:, :half_win], "win", -1)
            framed = jnp.concatenate([normed[:, half_win:], next_section], axis=1)
        complete = lax.all_gather(framed, "head", axis=2, tiled=True)
        attended = lax.cond(
            active,
            lambda pair: attend(pair[0], pair[1], query_scale, value_cols),
            lambda pair: jnp.zeros_like(pair[0]),
            (framed, complete),
        )
        if shifted:
            tail_cols = from_behind(attended[:, col_count - half_win :], "win", 1)
            attended = jnp.concatenate([tail_cols, attended[:, : col_count - half_win]], axis=1)
        term = lax.cond(
            active,
            lambda tensor: jnp.dot(
                tensor.reshape(row_count * col_count, channels),
                out_rows,
                preferred_element_type=jnp.float32,
            ).reshape(row_count, col_count, width_all),
            lambda tensor: jnp.zeros((row_count, col_count, width_all), jnp.float32),
            attended,
        )
        mixture = lax.psum_scatter(
            term.astype(jnp.bfloat16), "head", scatter_dimension=2, tiled=True
        ).astype(jnp.float32)
        updated = (current_f + mixture).astype(jnp.bfloat16)
        recorded = jnp.where(active, updated, recorded)
        if section + 1 < sections:
            current = from_behind_2(updated, "pipe", 1)
    return recorded[None]


def solution(mesh):
    placed = (
        P("head", "win", None),
        P("pipe", None),
        P("pipe", None, "head"),
        P("pipe", "head", None),
    )
    return jax.shard_map(
        per_device,
        mesh=mesh,
        in_specs=placed,
        out_specs=P("pipe", None, "win", "head"),
        check_vma=False,
    )
```

profile of v0, /device:TPU:16, one launch (start us, length us, event | category | flops | bytes accessed | tf_op | source)
XLA Modules:
  0.0 476.8 jit_solution(15864355350627802098)
XLA Ops:
  6.5 2.2 copy.69
  8.8 1.0 reshape.154
  9.7 10.8 %all_to_all.4 = bf16[4,2,16384]{2,1,0:T(2,128)(2,1)S(1)} all-to-all(bf16[4,2,16384]{2,1,0:T(2,128)(2,1)S(1)} %reshape.154), channel_id=1, replica_groups=mesh['pipe'=4,'win'=48,'head'=4] {'head'}, dimensions={0} | all-to-all | bytes 524288 | tf_op jit(solution)/shard_map/all_to_all | solution.py:68
  21.0 0.8 bitcast_convert_fusion
  21.8 1.4 bitcast_reduce_fusion
  23.2 0.9 copy.70
  24.2 8.9 %psum.28 = f32[8,32]{1,0:T(8,128)S(1)} all-reduce(f32[8,32]{1,0:T(8,128)S(1)} %bitcast.166), channel_id=1, replica_groups=mesh['pipe'=4,'win'=48,'head'=4] {'head'}, use_global_device_ids=true, to_apply=%region_1.0 | all-reduce | flops 256 | bytes 2048 | tf_op jit(solution)/shard_map/psum | solution.py:85
  33.1 0.8 fusion.37
  34.0 36.6 %all-gather.5.cloned.1.call-done = bf16[8,32,2048]{2,1,0:T(8,128)(2,1)} async-done(((bf16[8,32,512]{2,1,0:T(8,128)(2,1)}), bf16[8,32,2048]{2,1,0:T(8,128)(2,1)}) %all-gather.5.cloned.1.call-update) | async-done | bytes 1048592 | tf_op jit(solution)/shard_map/all_gather | solution.py:92
  70.6 0.7 conditional.8
  70.6 0.7 broadcast.50
  71.4 1.0 copy-done.1
  72.3 1.1 conditional.9
  72.3 1.1 broadcast.52
  73.5 40.7 %reduce-scatter.5.cloned.1.call-done = bf16[8,32,512]{2,1,0:T(8,128)(2,1)} async-done(((bf16[8,32,2048]{2,1,0:T(8,128)(2,1)}), bf16[8,32,512]{2,1,0:T(8,128)(2,1)}) %reduce-scatter.5.cloned.1.call-update) | async-done | bytes 262160 | tf_op jit(solution)/shard_map/reduce_scatter | solution.py:112
  114.2 1.0 fusion.38
  115.2 5.5 %collective-permute-start = (bf16[8,32,512]{2,1,0:T(8,128)(2,1)S(1)}, bf16[8,32,512]{2,1,0:T(8,128)(2,1)S(1)}, u32[]{:S(2)}, u32[]{:S(2)}) collective-permute-start(bf16[8,32,512]{2,1,0:T(8,128)(2,1)S(1)} %fusion.38), channel_id=1, source_target_pairs={{0,192},{192,384},{384,576},{1,193},{193,385},{385,577},{2,194},{1... | collective-permute-start | bytes 786440 | tf_op jit(solution)/shard_map/ppermute | solution.py:24
  120.8 9.6 %collective-permute-done = bf16[8,32,512]{2,1,0:T(8,128)(2,1)S(1)} collective-permute-done((bf16[8,32,512]{2,1,0:T(8,128)(2,1)S(1)}, bf16[8,32,512]{2,1,0:T(8,128)(2,1)S(1)}, u32[]{:S(2)}, u32[]{:S(2)}) %collective-permute-start) | collective-permute-done | bytes 262176 | tf_op jit(solution)/shard_map/ppermute | solution.py:24
  130.5 8.6 %psum.29 = f32[8,32]{1,0:T(8,128)S(1)} all-reduce(f32[8,32]{1,0:T(8,128)S(1)} %fusion.28), channel_id=1, replica_groups=mesh['pipe'=4,'win'=48,'head'=4] {'head'}, use_global_device_ids=true, to_apply=%region_10.11 | all-reduce | flops 256 | bytes 2048 | tf_op jit(solution)/shard_map/psum | solution.py:85
  139.2 5.0 %collective-permute-start.1 = (bf16[8,16,512]{2,1,0:T(8,128)(2,1)S(1)}, bf16[8,16,512]{2,1,0:T(8,128)(2,1)S(1)}, u32[]{:S(2)}, u32[]{:S(2)}) collective-permute-start(bf16[8,16,512]{2,1,0:T(8,128)(2,1)S(1)} %get-tuple-element.108), channel_id=1, source_target_pairs={{0,188},{4,0},{8,4},{12,8},{16,12},{20,16},{24,20},{28,24},{32,28}... | collective-permute-start | bytes 393224 | tf_op jit(solution)/shard_map/ppermute | solution.py:18
  144.2 2.5 collective-permute-done.1
  146.7 0.7 pad_maximum_fusion
  147.5 30.9 %all-gather.7.cloned.1.call-done = bf16[8,32,2048]{2,1,0:T(8,128)(2,1)} async-done(((bf16[8,32,512]{2,1,0:T(8,128)(2,1)}), bf16[8,32,2048]{2,1,0:T(8,128)(2,1)}) %all-gather.7.cloned.1.call-update) | async-done | bytes 1048592 | tf_op jit(solution)/shard_map/all_gather | solution.py:92
  178.5 16.5 %conditional.10 = (bf16[8,32,512]{2,1,0:T(8,128)(2,1)S(1)}) conditional(s32[]{:T(128)} %convert_element_type.161, () %tuple.58, (bf16[8,32,512]{2,1,0:T(8,128)(2,1)}, f32[512]{0:T(512)S(1)}, bf16[8,32,2048]{2,1,0:T(8,128)(2,1)}, bf16[2048,512]{1,0:T(8,128)(2,1)}) %tuple.114), branch_computations={%region_11.12_spmd, %region_12.15_spmd} | conditional | flops 740689408 | bytes 12855332 | solution.py:93
  178.5 1.0 multiply_convert_fusion.1
  179.5 0.8 copy.54
  180.3 1.0 reshape.123
  181.4 0.7 copy-done.10
  182.0 1.2 convolution_multiply_fusion.1
  183.3 1.5 fusion.42
  184.8 3.3 convolution_convert_fusion.3
  188.1 1.7 reshape.126
  189.9 1.7 copy.56
  191.6 2.1 convolution_convert_fusion.2
  193.7 1.2 copy.58
  195.0 1.9 collective-permute-start.2
  196.9 6.5 %collective-permute-done.2 = bf16[8,16,512]{2,1,0:T(8,128)(2,1)S(1)} collective-permute-done((bf16[8,16,512]{2,1,0:T(8,128)(2,1)S(1)}, bf16[8,16,512]{2,1,0:T(8,128)(2,1)S(1)}, u32[]{:S(2)}, u32[]{:S(2)}) %collective-permute-start.2) | collective-permute-done | bytes 131104 | tf_op jit(solution)/shard_map/ppermute | solution.py:18
  203.4 0.7 pad_maximum_fusion.1
  204.1 1.7 conditional.11
  204.1 1.7 fusion.12
  205.8 1.0 copy-done.4
  206.9 28.1 %reduce-scatter.7.cloned.1.call-done = bf16[8,32,512]{2,1,0:T(8,128)(2,1)} async-done(((bf16[8,32,2048]{2,1,0:T(8,128)(2,1)}), bf16[8,32,512]{2,1,0:T(8,128)(2,1)}) %reduce-scatter.7.cloned.1.call-update) | async-done | bytes 262160 | tf_op jit(solution)/shard_map/reduce_scatter | solution.py:112
  234.9 1.0 fusion.30
  236.0 5.5 %collective-permute-start.3 = (bf16[8,32,512]{2,1,0:T(8,128)(2,1)S(1)}, bf16[8,32,512]{2,1,0:T(8,128)(2,1)S(1)}, u32[]{:S(2)}, u32[]{:S(2)}) collective-permute-start(bf16[8,32,512]{2,1,0:T(8,128)(2,1)S(1)} %fusion.30), channel_id=1, source_target_pairs={{0,192},{192,384},{384,576},{1,193},{193,385},{385,577},{2,194},{1... | collective-permute-start | bytes 786440 | tf_op jit(solution)/shard_map/ppermute | solution.py:24
  241.5 9.7 %collective-permute-done.3 = bf16[8,32,512]{2,1,0:T(8,128)(2,1)S(1)} collective-permute-done((bf16[8,32,512]{2,1,0:T(8,128)(2,1)S(1)}, bf16[8,32,512]{2,1,0:T(8,128)(2,1)S(1)}, u32[]{:S(2)}, u32[]{:S(2)}) %collective-permute-start.3) | collective-permute-done | bytes 262176 | tf_op jit(solution)/shard_map/ppermute | solution.py:24
  251.3 8.6 %psum.30 = f32[8,32]{1,0:T(8,128)S(1)} all-reduce(f32[8,32]{1,0:T(8,128)S(1)} %fusion.31), channel_id=1, replica_groups=mesh['pipe'=4,'win'=48,'head'=4] {'head'}, use_global_device_ids=true, to_apply=%region_19.20 | all-reduce | flops 256 | bytes 2048 | tf_op jit(solution)/shard_map/psum | solution.py:85
  259.9 0.8 fusion.32
  260.8 32.8 %all-gather.9.cloned.1.call-done = bf16[8,32,2048]{2,1,0:T(8,128)(2,1)} async-done(((bf16[8,32,512]{2,1,0:T(8,128)(2,1)}), bf16[8,32,2048]{2,1,0:T(8,128)(2,1)}) %all-gather.9.cloned.1.call-update) | async-done | bytes 1048592 | tf_op jit(solution)/shard_map/all_gather | solution.py:92
  293.9 1.0 copy-done.5
  295.0 50.9 %reduce-scatter.9.cloned.1.call-done = bf16[8,32,512]{2,1,0:T(8,128)(2,1)} async-done(((bf16[8,32,2048]{2,1,0:T(8,128)(2,1)}), bf16[8,32,512]{2,1,0:T(8,128)(2,1)}) %reduce-scatter.9.cloned.1.call-update) | async-done | bytes 262160 | tf_op jit(solution)/shard_map/reduce_scatter | solution.py:112
  345.9 1.0 fusion.33
  347.0 5.5 %collective-permute-start.4 = (bf16[8,32,512]{2,1,0:T(8,128)(2,1)S(1)}, bf16[8,32,512]{2,1,0:T(8,128)(2,1)S(1)}, u32[]{:S(2)}, u32[]{:S(2)}) collective-permute-start(bf16[8,32,512]{2,1,0:T(8,128)(2,1)S(1)} %fusion.33), channel_id=1, source_target_pairs={{0,192},{192,384},{384,576},{1,193},{193,385},{385,577},{2,194},{1... | collective-permute-start | bytes 786440 | tf_op jit(solution)/shard_map/ppermute | solution.py:24
  352.5 9.6 %collective-permute-done.4 = bf16[8,32,512]{2,1,0:T(8,128)(2,1)S(1)} collective-permute-done((bf16[8,32,512]{2,1,0:T(8,128)(2,1)S(1)}, bf16[8,32,512]{2,1,0:T(8,128)(2,1)S(1)}, u32[]{:S(2)}, u32[]{:S(2)}) %collective-permute-start.4) | collective-permute-done | bytes 262176 | tf_op jit(solution)/shard_map/ppermute | solution.py:24
  362.2 8.6 %psum.31 = f32[8,32]{1,0:T(8,128)S(1)} all-reduce(f32[8,32]{1,0:T(8,128)S(1)} %fusion.34), channel_id=1, replica_groups=mesh['pipe'=4,'win'=48,'head'=4] {'head'}, use_global_device_ids=true, to_apply=%region_28.29 | all-reduce | flops 256 | bytes 2048 | tf_op jit(solution)/shard_map/psum | solution.py:85
  371.0 5.0 %collective-permute-start.5 = (bf16[8,16,512]{2,1,0:T(8,128)(2,1)S(1)}, bf16[8,16,512]{2,1,0:T(8,128)(2,1)S(1)}, u32[]{:S(2)}, u32[]{:S(2)}) collective-permute-start(bf16[8,16,512]{2,1,0:T(8,128)(2,1)S(1)} %get-tuple-element.104), channel_id=1, source_target_pairs={{0,188},{4,0},{8,4},{12,8},{16,12},{20,16},{24,20},{28,24},{32,28}... | collective-permute-start | bytes 393224 | tf_op jit(solution)/shard_map/ppermute | solution.py:18
  375.9 2.5 collective-permute-done.5
  378.4 0.7 pad_maximum_fusion.2
  379.2 31.0 %all-gather.11.cloned.1.call-done = bf16[8,32,2048]{2,1,0:T(8,128)(2,1)} async-done(((bf16[8,32,512]{2,1,0:T(8,128)(2,1)}), bf16[8,32,2048]{2,1,0:T(8,128)(2,1)}) %all-gather.11.cloned.1.call-update) | async-done | bytes 1048592 | tf_op jit(solution)/shard_map/all_gather | solution.py:92
  410.3 1.9 collective-permute-start.6
  412.2 6.5 %collective-permute-done.6 = bf16[8,16,512]{2,1,0:T(8,128)(2,1)S(1)} collective-permute-done((bf16[8,16,512]{2,1,0:T(8,128)(2,1)S(1)}, bf16[8,16,512]{2,1,0:T(8,128)(2,1)S(1)}, u32[]{:S(2)}, u32[]{:S(2)}) %collective-permute-start.6) | collective-permute-done | bytes 131104 | tf_op jit(solution)/shard_map/ppermute | solution.py:18
  418.7 0.7 pad_maximum_fusion.3
  419.5 1.0 copy-done.6
  420.5 47.5 %reduce-scatter.11.cloned.1.call-done = bf16[8,32,512]{2,1,0:T(8,128)(2,1)} async-done(((bf16[8,32,2048]{2,1,0:T(8,128)(2,1)}), bf16[8,32,512]{2,1,0:T(8,128)(2,1)}) %reduce-scatter.11.cloned.1.call-update) | async-done | bytes 262160 | tf_op jit(solution)/shard_map/reduce_scatter | solution.py:112
  468.1 1.8 fusion.40
  (61 shorter events, 2.8 us)
Async XLA Ops:
  6.5 27.5 %copy-start = (f32[1,2048]{1,0:T(1,128)S(1)}, f32[1,2048]{1,0:T(1,128)}, u32[]{:S(2)}) copy-start(f32[1,2048]{1,0:T(1,128)} %param.21) | copy-start | bytes 24580
  6.5 64.1 %all-gather.5.cloned.1.call-start = ((), (), s32[]{:S(2)}) async-start(), calls=%async_computation.5 | async-start | bytes 1310720 | tf_op jit(solution)/shard_map/all_gather | solution.py:92
  24.0 46.6 %copy-start.2 = (f32[4,2,32,512]{3,2,1,0:T(8,128)}, f32[4,2,32,512]{3,2,1,0:T(8,128)S(1)}, u32[]{:S(2)}) copy-start(f32[4,2,32,512]{3,2,1,0:T(8,128)S(1)} %copy.70) | copy-start | bytes 1572868
  33.9 80.2 %reduce-scatter.5.cloned.1.call-start = ((), (), s32[]{:S(2)}) async-start(), calls=%async_computation.6 | async-start | bytes 1310720 | tf_op jit(solution)/shard_map/reduce_scatter | solution.py:112
  70.6 1.7 copy-start.1
  72.3 41.9 %copy-start.3 = (f32[4,2,32,512]{3,2,1,0:T(8,128)S(1)}, f32[4,2,32,512]{3,2,1,0:T(8,128)}, u32[]{:S(2)}) copy-start(f32[4,2,32,512]{3,2,1,0:T(8,128)} %copy-done.2) | copy-start | bytes 1572868
  73.5 105.0 %all-gather.7.cloned.1.call-start = ((), (), s32[]{:S(2)}) async-start(), calls=%async_computation.7 | async-start | bytes 1310720 | tf_op jit(solution)/shard_map/all_gather | solution.py:92
  115.2 63.2 %copy-start.13 = (bf16[8,32,512]{2,1,0:T(8,128)(2,1)}, bf16[8,32,512]{2,1,0:T(8,128)(2,1)S(1)}, u32[]{:S(2)}) copy-start(bf16[8,32,512]{2,1,0:T(8,128)(2,1)S(1)} %fusion.38) | copy-start | bytes 786436
  115.2 15.1 %collective-permute-start = (bf16[8,32,512]{2,1,0:T(8,128)(2,1)S(1)}, bf16[8,32,512]{2,1,0:T(8,128)(2,1)S(1)}, u32[]{:S(2)}, u32[]{:S(2)}) collective-permute-start(bf16[8,32,512]{2,1,0:T(8,128)(2,1)S(1)} %fusion.38), channel_id=1, source_target_pairs={{0,192},{192,384},{384,576},{1,193},{193,385},{385,577},{2,194},{1... | collective-permute-start | bytes 786440 | tf_op jit(solution)/shard_map/ppermute | solution.py:24
  139.2 7.5 %collective-permute-start.1 = (bf16[8,16,512]{2,1,0:T(8,128)(2,1)S(1)}, bf16[8,16,512]{2,1,0:T(8,128)(2,1)S(1)}, u32[]{:S(2)}, u32[]{:S(2)}) collective-permute-start(bf16[8,16,512]{2,1,0:T(8,128)(2,1)S(1)} %get-tuple-element.108), channel_id=1, source_target_pairs={{0,188},{4,0},{8,4},{12,8},{16,12},{20,16},{24,20},{28,24},{32,28}... | collective-permute-start | bytes 393224 | tf_op jit(solution)/shard_map/ppermute | solution.py:18
  147.5 87.5 %reduce-scatter.7.cloned.1.call-start = ((), (), s32[]{:S(2)}) async-start(), calls=%async_computation.8 | async-start | bytes 1310720 | tf_op jit(solution)/shard_map/reduce_scatter | solution.py:112
  181.3 0.7 copy-start.10
  195.0 8.4 %collective-permute-start.2 = (bf16[8,16,512]{2,1,0:T(8,128)(2,1)S(1)}, bf16[8,16,512]{2,1,0:T(8,128)(2,1)S(1)}, u32[]{:S(2)}, u32[]{:S(2)}) collective-permute-start(bf16[8,16,512]{2,1,0:T(8,128)(2,1)S(1)} %get-tuple-element.105), channel_id=1, source_target_pairs={{0,4},{4,8},{8,12},{12,16},{16,20},{20,24},{24,28},{28,32},{32,36}... | collective-permute-start | bytes 393224 | tf_op jit(solution)/shard_map/ppermute | solution.py:18
  205.8 1.0 copy-start.4
  206.8 86.8 %all-gather.9.cloned.1.call-start = ((), (), s32[]{:S(2)}) async-start(), calls=%async_computation.9 | async-start | bytes 1310720 | tf_op jit(solution)/shard_map/all_gather | solution.py:92
  235.9 57.6 %copy-start.7 = (bf16[8,32,512]{2,1,0:T(8,128)(2,1)}, bf16[8,32,512]{2,1,0:T(8,128)(2,1)S(1)}, u32[]{:S(2)}) copy-start(bf16[8,32,512]{2,1,0:T(8,128)(2,1)S(1)} %fusion.30) | copy-start | bytes 786436
  236.0 15.2 %collective-permute-start.3 = (bf16[8,32,512]{2,1,0:T(8,128)(2,1)S(1)}, bf16[8,32,512]{2,1,0:T(8,128)(2,1)S(1)}, u32[]{:S(2)}, u32[]{:S(2)}) collective-permute-start(bf16[8,32,512]{2,1,0:T(8,128)(2,1)S(1)} %fusion.30), channel_id=1, source_target_pairs={{0,192},{192,384},{384,576},{1,193},{193,385},{385,577},{2,194},{1... | collective-permute-start | bytes 786440 | tf_op jit(solution)/shard_map/ppermute | solution.py:24
  260.7 85.2 %reduce-scatter.9.cloned.1.call-start = ((), (), s32[]{:S(2)}) async-start(), calls=%async_computation.10 | async-start | bytes 1310720 | tf_op jit(solution)/shard_map/reduce_scatter | solution.py:112
  293.9 1.0 copy-start.5
  294.9 115.3 %all-gather.11.cloned.1.call-start = ((), (), s32[]{:S(2)}) async-start(), calls=%async_computation.11 | async-start | bytes 1310720 | tf_op jit(solution)/shard_map/all_gather | solution.py:92
  347.0 63.3 %copy-start.8 = (bf16[8,32,512]{2,1,0:T(8,128)(2,1)}, bf16[8,32,512]{2,1,0:T(8,128)(2,1)S(1)}, u32[]{:S(2)}) copy-start(bf16[8,32,512]{2,1,0:T(8,128)(2,1)S(1)} %fusion.33) | copy-start | bytes 786436
  347.0 15.1 %collective-permute-start.4 = (bf16[8,32,512]{2,1,0:T(8,128)(2,1)S(1)}, bf16[8,32,512]{2,1,0:T(8,128)(2,1)S(1)}, u32[]{:S(2)}, u32[]{:S(2)}) collective-permute-start(bf16[8,32,512]{2,1,0:T(8,128)(2,1)S(1)} %fusion.33), channel_id=1, source_target_pairs={{0,192},{192,384},{384,576},{1,193},{193,385},{385,577},{2,194},{1... | collective-permute-start | bytes 786440 | tf_op jit(solution)/shard_map/ppermute | solution.py:24
  371.0 7.5 %collective-permute-start.5 = (bf16[8,16,512]{2,1,0:T(8,128)(2,1)S(1)}, bf16[8,16,512]{2,1,0:T(8,128)(2,1)S(1)}, u32[]{:S(2)}, u32[]{:S(2)}) collective-permute-start(bf16[8,16,512]{2,1,0:T(8,128)(2,1)S(1)} %get-tuple-element.104), channel_id=1, source_target_pairs={{0,188},{4,0},{8,4},{12,8},{16,12},{20,16},{24,20},{28,24},{32,28}... | collective-permute-start | bytes 393224 | tf_op jit(solution)/shard_map/ppermute | solution.py:18
  379.2 88.9 %reduce-scatter.11.cloned.1.call-start = ((), (), s32[]{:S(2)}) async-start(), calls=%async_computation.12 | async-start | bytes 1310720 | tf_op jit(solution)/shard_map/reduce_scatter | solution.py:112
  410.3 8.4 %collective-permute-start.6 = (bf16[8,16,512]{2,1,0:T(8,128)(2,1)S(1)}, bf16[8,16,512]{2,1,0:T(8,128)(2,1)S(1)}, u32[]{:S(2)}, u32[]{:S(2)}) collective-permute-start(bf16[8,16,512]{2,1,0:T(8,128)(2,1)S(1)} %get-tuple-element.101), channel_id=1, source_target_pairs={{0,4},{4,8},{8,12},{12,16},{16,20},{20,24},{24,28},{28,32},{32,36}... | collective-permute-start | bytes 393224 | tf_op jit(solution)/shard_map/ppermute | solution.py:18
  419.5 1.0 copy-start.6
Sparse Core Ops, SparseCore 0:
  34.1 36.5 all-gather.4
  73.8 40.3 reduce-scatter.4
  147.6 30.8 all-gather.6
  206.9 27.9 reduce-scatter.6
  260.8 32.6 all-gather.8
  296.5 49.3 reduce-scatter.8
  379.3 30.8 all-gather.10
  420.7 47.3 reduce-scatter.10
where the time goes:
time: 478 us; the launch traced here: 477 us
  waiting for transfers between devices  345 us (72%)
  blocking collectives  45.4 us (9%)
  starting transfers between devices  30.6 us (6%)
  local copies, waits for them, and re-layouts  18.1 us (4%)
  between operations  13.8 us (3%)
  other arithmetic  13.2 us (3%)
  matrix products  9.9 us (2%)
    reduce_scatter x4, waiting for transfers between devices, per_device(): lax.psum_scatter(term.astype(jnp.bfloat16), 'head', scatter_dimension=2,...  167 us
    all_gather x4, waiting for transfers between devices, per_device(): complete = lax.all_gather(framed, 'head', axis=2, tiled=True)  131 us
    psum x4, blocking collectives, per_device(): square_sums = lax.psum(partial_value, 'head')  34.6 us
    ppermute x3, waiting for transfers between devices, from_behind_2(): lax.ppermute(value, axis, [(source, source + steps) for source in range(l...  28.8 us
    ppermute x4, waiting for transfers between devices, from_behind(): return lax.ppermute(value, axis, pairs)  17.9 us
    ppermute x3, starting transfers between devices, from_behind_2(): lax.ppermute(value, axis, [(source, source + steps) for source in range(l...  16.6 us
    ppermute x4, starting transfers between devices, from_behind(): return lax.ppermute(value, axis, pairs)  13.8 us
    all_to_all x1, blocking collectives, per_device(): lax.all_to_all(stream, 'head', split_axis=2, concat_axis=0, tiled=True)  10.8 us
  transfers between devices with their start and end apart: 15, of which 15 were waited for; matrix products, arithmetic and copies ran while one was open for 0% of the time, Pallas kernels for 0%

commit v1 on v0

v1 whole, which is shorter than its diff:
```python
import functools
import math

import jax
import jax.numpy as jnp
from jax import lax
from jax.experimental import pallas as pl
from jax.experimental.pallas import tpu as pltpu
from jax.sharding import PartitionSpec as P

MESH = pl.DeviceIdType.MESH
HEAD_DIM = 128
EPSILON = 1e-06
BF16, F32 = jnp.bfloat16, jnp.float32

CHUNKS = 4
RIGHT, LEFT = 0, 1


def kernel(
    sizes, stream, scale, wv_hbm, wo_hbm, out,
    xin, wv, wo, ubuf, vbuf, obuf, g2, r2, gown, gside, gsend, grecv, xnew,
    w_sem, own_sem, ag_s, ag_r, rl_s, rl_r, r2_s, r2_r, rs_s, rs_r, pp_s, pp_r, os_s, os_r, out_sem,
):
    n_pipe, n_win, n_head = sizes
    rows, half_cols, width = xin.shape[1:]
    cut = width // n_head
    heads = cut // HEAD_DIM
    per_half = CHUNKS // 2
    crows = rows // per_half
    cells = crows * half_cols
    my_rows = stream.shape[0]
    p, w, h = lax.axis_index("pipe"), lax.axis_index("win"), lax.axis_index("head")
    odd = lax.rem(p, 2)
    right, left, far = lax.rem(h + 1, n_head), lax.rem(h + n_head - 1, n_head), lax.rem(h + 2, n_head)
    w_next, w_prev = lax.rem(w + 1, n_win), lax.rem(w + n_win - 1, n_win)
    w_to = lax.rem(w + n_win - 1 + 2 * odd, n_win)
    w_from = lax.rem(w + n_win - 1 + 2 * odd, n_win)
    side = ((p, w, right), (p, w, left))

    def lanes(k):
        return pl.ds(pl.multiple_of(k * cut, cut), cut)

    def remote(src, dst, s_sem, r_sem, to):
        return pltpu.make_async_remote_copy(
            src_ref=src, dst_ref=dst, send_sem=s_sem, recv_sem=r_sem, device_id=to, device_id_type=MESH)

    load_v = pltpu.make_async_copy(wv_hbm.at[0], wv, w_sem.at[0])
    load_o = pltpu.make_async_copy(wo_hbm.at[0], wo, w_sem.at[1])

    barrier = pltpu.get_barrier_semaphore()

    def greet(to):
        pl.semaphore_signal(barrier, inc=1, device_id=to, device_id_type=MESH)

    greet(side[RIGHT])
    greet(side[LEFT])

    @pl.when(p > 0)
    def _():
        greet((p - 1, w, h))
        greet((p - 1, w_from, h))

    @pl.when(odd == 1)
    def _():
        greet((p, w_prev, h))

    @pl.when(p > 0)
    def _():
        load_v.start()
        load_o.start()

    for k in range(n_pipe):
        @pl.when(p == k)
        def _():
            pl.semaphore_wait(barrier, 2 + 2 * (k < n_pipe - 1) + k % 2)

    def place(c):
        return c // per_half, (c % per_half) * crows

    def normalize(c):
        a, r0 = place(c)
        x = xin[a, r0:r0 + crows].reshape(cells, width).astype(F32)
        inverse = lax.rsqrt(jnp.sum(x * x, axis=1, keepdims=True) * (1.0 / width) + EPSILON)
        u = (x * inverse).astype(BF16)
        mine = xin[a, r0:r0 + crows, :, lanes(h)].reshape(cells, cut).astype(F32)
        ubuf[c * cells:(c + 1) * cells, :] = (mine * inverse).astype(BF16)
        vbuf[c * cells:(c + 1) * cells, :] = jnp.dot(u, wv[...], preferred_element_type=F32).astype(BF16)

    @pl.when(p == 0)
    def _():
        def rows_of(k):
            return pl.ds(k * my_rows, my_rows)

        def spread(a, d):
            return remote(
                stream.at[:, pl.ds(a * half_cols, half_cols)], xin.at[a, rows_of(h)],
                ag_s.at[d, a], ag_r.at[d, a], side[d])

        def relay(a, d):
            row = (left if d == RIGHT else right) * my_rows + d
            part = xin.at[a, pl.ds(row, 1)]
            return remote(part, part, rl_s.at[d, a], rl_r.at[d, a], side[d])

        own = [
            pltpu.make_async_copy(
                stream.at[:, pl.ds(a * half_cols, half_cols)], xin.at[a, rows_of(h)], own_sem.at[a])
            for a in range(2)
        ]
        for a in range(2):
            for d in (RIGHT, LEFT):
                spread(a, d).start()
            own[a].start()
        load_v.start()
        load_o.start()
        for a in range(2):
            for d in (RIGHT, LEFT):
                spread(a, d).wait_recv()
                relay(a, d).start()
        load_v.wait()
        for a in range(2):
            own[a].wait()
            for d in (RIGHT, LEFT):
                relay(a, d).wait_recv()
            for c in range(a * per_half, (a + 1) * per_half):
                normalize(c)
        for a in range(2):
            for d in (RIGHT, LEFT):
                spread(a, d).wait_send()
                relay(a, d).wait_send()

    def hand_on(c):
        a, r0 = place(c)
        to = (p + 1, w_to if a == 0 else w, h)
        return remote(
            xnew.at[a, pl.ds(r0, crows)], xin.at[a, pl.ds(r0, crows), :, lanes(h)],
            pp_s.at[c], pp_r.at[c], to)

    @pl.when(p > 0)
    def _():
        def spread(c, d):
            a, r0 = place(c)
            part = xin.at[a, pl.ds(r0, crows), :, lanes(h)]
            return remote(part, part, ag_s.at[d, c], ag_r.at[d, c], side[d])

        def relay(c, d):
            a, r0 = place(c)
            part = xin.at[a, pl.ds(r0 + d * (crows // 2), crows // 2), :, lanes(left if d == RIGHT else right)]
            return remote(part, part, rl_s.at[d, c], rl_r.at[d, c], side[d])

        load_v.wait()
        for i in range(CHUNKS + 2):
            if i < CHUNKS:
                hand_on(i).wait_recv()
                for d in (RIGHT, LEFT):
                    spread(i, d).start()
            if 1 <= i <= CHUNKS:
                for d in (RIGHT, LEFT):
                    spread(i - 1, d).wait_recv()
                    relay(i - 1, d).start()
            if i >= 2:
                for d in (RIGHT, LEFT):
                    relay(i - 2, d).wait_recv()
                normalize(i - 2)
        for c in range(CHUNKS):
            for d in (RIGHT, LEFT):
                spread(c, d).wait_send()
                relay(c, d).wait_send()

    load_o.wait()
    inv_root = 1.0 / math.sqrt(HEAD_DIM)

    def attend(c):
        for j in range(heads):
            col = slice(j * HEAD_DIM, (j + 1) * HEAD_DIM)
            gain = scale[:, pl.ds(pl.multiple_of(h * cut + j * HEAD_DIM, HEAD_DIM), HEAD_DIM)]
            q = (ubuf[c * cells:(c + 1) * cells, col].astype(F32) * gain).astype(BF16)
            s = lax.dot_general(q, ubuf[:, col], (((1,), (1,)), ((), ())), preferred_element_type=F32) * inv_root
            e = jnp.exp(s - jnp.max(s, axis=1, keepdims=True))
            prob = (e / jnp.sum(e, axis=1, keepdims=True)).astype(BF16)
            obuf[c, :, col] = jnp.dot(prob, vbuf[:, col], preferred_element_type=F32).astype(BF16)

    def project(c, k):
        return jnp.dot(obuf[c], wo[:, lanes(k)], preferred_element_type=F32)

    half_cells = cells // 2

    def far_share(c, d):
        rows_ = pl.ds(d * half_cells, half_cells)
        return remote(g2.at[c, rows_], r2.at[c, d], r2_s.at[d, c], r2_r.at[d, c], side[d])

    def near_share(c, d):
        return remote(gsend.at[c, d], grecv.at[c, d], rs_s.at[d, c], rs_r.at[d, c], side[d])

    def cols_of(a):
        return pl.ds(a * half_cols, half_cols)

    def keep(c):
        a, r0 = place(c)
        return pltpu.make_async_copy(
            xnew.at[a, pl.ds(r0, crows)], out.at[0, pl.ds(r0, crows), cols_of(a)], out_sem.at[c])

    def keep_next(c):
        a, r0 = place(c)
        return remote(
            xnew.at[a, pl.ds(r0, crows)], out.at[0, pl.ds(r0, crows), cols_of(a)],
            os_s.at[c], os_r.at[c], (p, w_next, h))

    for i in range(CHUNKS + 2):
        if i < CHUNKS:
            c = i
            attend(c)
            g2[c] = project(c, far).astype(BF16)
            for d in (RIGHT, LEFT):
                far_share(c, d).start()
            gside[c, RIGHT] = project(c, right)
            gside[c, LEFT] = project(c, left)
            gown[c] = project(c, h)
        if 1 <= i <= CHUNKS:
            c = i - 1
            for d in (RIGHT, LEFT):
                far_share(c, d).wait_recv()
                first = d * half_cells
                rest = (1 - d) * half_cells
                gsend[c, d, first:first + half_cells] = (
                    gside[c, d, first:first + half_cells] + r2[c, d].astype(F32)).astype(BF16)
                gsend[c, d, rest:rest + half_cells] = gside[c, d, rest:rest + half_cells].astype(BF16)
                near_share(c, d).start()
        if i >= 2:
            c = i - 2
            a, r0 = place(c)
            total = xin[a, r0:r0 + crows, :, lanes(h)].reshape(cells, cut).astype(F32) + gown[c]
            for d in (RIGHT, LEFT):
                near_share(c, d).wait_recv()
                total = total + grecv[c, d].astype(F32)
            xnew[a, r0:r0 + crows] = total.astype(BF16).reshape(crows, half_cols, cut)

            @pl.when(p < n_pipe - 1)
            def _():
                hand_on(c).start()

            if a == 1:
                keep(c).start()
            else:
                @pl.when(odd == 0)
                def _():
                    keep(c).start()

                @pl.when(odd == 1)
                def _():
                    keep_next(c).start()

    for c in range(CHUNKS):
        for d in (RIGHT, LEFT):
            far_share(c, d).wait_send()
            near_share(c, d).wait_send()

        @pl.when(p < n_pipe - 1)
        def _():
            hand_on(c).wait_send()

        if place(c)[0] == 1:
            keep(c).wait()
        else:
            @pl.when(odd == 0)
            def _():
                keep(c).wait()

            @pl.when(odd == 1)
            def _():
                keep_next(c).wait_send()
                keep_next(c).wait_recv()


def solution(mesh):
    sizes = tuple(mesh.shape[name] for name in ("pipe", "win", "head"))

    def per_device(stream, score_scale, value_weight, out_weight):
        my_rows, cols, width = stream.shape
        rows, half_cols, cut = my_rows * sizes[2], cols // 2, width // sizes[2]
        cells = rows * cols // CHUNKS
        anywhere = pl.BlockSpec(memory_space=pl.ANY)
        dma = pltpu.SemaphoreType.DMA
        return pl.pallas_call(
            functools.partial(kernel, sizes),
            out_shape=jax.ShapeDtypeStruct((1, rows, cols, cut), BF16),
            in_specs=[anywhere, pl.BlockSpec(memory_space=pltpu.VMEM), anywhere, anywhere],
            out_specs=anywhere,
            scratch_shapes=[
                pltpu.VMEM((2, rows, half_cols, width), BF16),
                pltpu.VMEM((width, cut), BF16),
                pltpu.VMEM((cut, width), BF16),
                pltpu.VMEM((rows * cols, cut), BF16),
                pltpu.VMEM((rows * cols, cut), BF16),
                pltpu.VMEM((CHUNKS, cells, cut), BF16),
                pltpu.VMEM((CHUNKS, cells, cut), BF16),
                pltpu.VMEM((CHUNKS, 2, cells // 2, cut), BF16),
                pltpu.VMEM((CHUNKS, cells, cut), F32),
                pltpu.VMEM((CHUNKS, 2, cells, cut), F32),
                pltpu.VMEM((CHUNKS, 2, cells, cut), BF16),
                pltpu.VMEM((CHUNKS, 2, cells, cut), BF16),
                pltpu.VMEM((2, rows, half_cols, cut), BF16),
                dma((2,)), dma((2,)),
                dma((2, CHUNKS)), dma((2, CHUNKS)),
                dma((2, CHUNKS)), dma((2, CHUNKS)),
                dma((2, CHUNKS)), dma((2, CHUNKS)),
                dma((2, CHUNKS)), dma((2, CHUNKS)),
                dma((CHUNKS,)), dma((CHUNKS,)),
                dma((CHUNKS,)), dma((CHUNKS,)),
                dma((CHUNKS,)),
            ],
            compiler_params=pltpu.CompilerParams(collective_id=0, has_side_effects=True),
        )(stream, score_scale, value_weight, out_weight)

    return jax.shard_map(
        per_device,
        mesh=mesh,
        in_specs=(P("head", "win", None), P("pipe", None), P("pipe", None, "head"), P("pipe", "head", None)),
        out_specs=P("pipe", None, "win", "head"),
        check_vma=False,
    )
```

time: 478 us -> 138 us (0.29)
  the two profiles are of different devices: /device:TPU:16 before, /device:TPU:50 now
where the time goes in v1:
time: 138 us
  Pallas kernels  136 us (99%)
  local copies, waits for them, and re-layouts  1.67 us (1%)
    pallas_call x1, Pallas kernels, per_device(): pl.pallas_call(functools.partial(kernel, sizes), out_shape=jax.ShapeDtype...  136 us

profile of v1, /device:TPU:50, one launch (start us, length us, event | category | flops | bytes accessed | tf_op | source)
XLA Modules:
  0.0 138.0 jit_solution(2261625821802945100)
XLA Ops:
  0.0 136.3 %shard_map.46 = bf16[1,8,32,512]{3,2,1,0:T(8,128)(2,1)} custom-call(bf16[2,32,2048]{2,1,0:T(8,128)(2,1)} %stream.1, f32[1,2048]{1,0:T(1,128)} %scale.1, bf16[1,2048,512]{2,1,0:T(8,128)(2,1)} %wv_hbm.1, bf16[1,512,2048]{2,1,0:T(8,128)(2,1)} %wo_hbm.1), custom_call_target="tpu_custom_call" | custom-call | tf_op jit(solution)/shard_map/pallas_call | solution.py:284
  136.3 1.7 %copy.6 = bf16[1,8,32,512]{3,2,1,0:T(8,128)(2,1)} copy(bf16[1,8,32,512]{3,2,1,0:T(8,128)(2,1)} %shard_map.46) | data formatting | bytes 524288

commit v2 on v1

--- a/solution.py
+++ b/solution.py
@@ -13,7 +13,7 @@
 EPSILON = 1e-06
 BF16, F32 = jnp.bfloat16, jnp.float32
 
-CHUNKS = 4
+CHUNKS = 8
 RIGHT, LEFT = 0, 1
 
 

time: 138 us -> 175 us (1.27)
  Pallas kernels: 136 us -> 174 us
    pallas_call x1, Pallas kernels: 136 us -> 174 us  [per_device(): pl.pallas_call(functools.partial(kernel, sizes), out_shape=jax.ShapeDtype...]
where the time goes in v2:
time: 175 us
  Pallas kernels  174 us (99%)
    pallas_call x1, Pallas kernels, per_device(): pl.pallas_call(functools.partial(kernel, sizes), out_shape=jax.ShapeDtype...  174 us

profile of v2, /device:TPU:50, one launch (start us, length us, event | category | flops | bytes accessed | tf_op | source)
XLA Modules:
  0.0 175.2 jit_solution(15490443190888476494)
XLA Ops:
  0.0 173.5 %shard_map.46 = bf16[1,8,32,512]{3,2,1,0:T(8,128)(2,1)} custom-call(bf16[2,32,2048]{2,1,0:T(8,128)(2,1)} %stream.1, f32[1,2048]{1,0:T(1,128)} %scale.1, bf16[1,2048,512]{2,1,0:T(8,128)(2,1)} %wv_hbm.1, bf16[1,512,2048]{2,1,0:T(8,128)(2,1)} %wo_hbm.1), custom_call_target="tpu_custom_call" | custom-call | tf_op jit(solution)/shard_map/pallas_call | solution.py:284
  173.6 1.7 copy.6

commit v3 on v2

v3 whole, which is shorter than its diff:
```python
import functools
import math

import jax
import jax.numpy as jnp
from jax import lax
from jax.experimental import pallas as pl
from jax.experimental.pallas import tpu as pltpu
from jax.sharding import PartitionSpec as P

MESH = pl.DeviceIdType.MESH
HEAD_DIM = 128
EPSILON = 1e-06
BF16, F32 = jnp.bfloat16, jnp.float32

CHUNKS = ((0, 0, 1), (0, 1, 2), (0, 3, 2), (0, 5, 3), (1, 0, 3), (1, 3, 2), (1, 5, 2), (1, 7, 1))
COUNT = len(CHUNKS)
FIRST_OF_1 = next(c for c in range(COUNT) if CHUNKS[c][0] == 1)
RIGHT, LEFT = 0, 1


def kernel(
    sizes, stream, scale, wv_hbm, wo_hbm, out,
    xin, wv, wo, ubuf, vbuf, obuf, g2, r2, rfar, gown, gside, gsend, grecv, xnew,
    w_sem, own_sem, ag_s, ag_r, rl_s, rl_r, r2_s, r2_r, rs_s, rs_r, pp_s, pp_r, os_s, os_r, out_sem,
):
    n_pipe, n_win, n_head = sizes
    rows, half_cols, width = xin.shape[1:]
    cut = width // n_head
    half_cut = cut // 2
    heads = cut // HEAD_DIM
    half = rows * half_cols
    my_rows = stream.shape[0]
    p, w, h = lax.axis_index("pipe"), lax.axis_index("win"), lax.axis_index("head")
    odd = lax.rem(p, 2)
    right, left, far = lax.rem(h + 1, n_head), lax.rem(h + n_head - 1, n_head), lax.rem(h + 2, n_head)
    w_next, w_prev = lax.rem(w + 1, n_win), lax.rem(w + n_win - 1, n_win)
    w_to = lax.rem(w + n_win - 1 + 2 * odd, n_win)
    w_from = lax.rem(w + n_win - 1 + 2 * odd, n_win)
    side = ((p, w, right), (p, w, left))
    across = (p, w, far)

    def lanes(k):
        return pl.ds(pl.multiple_of(k * cut, cut), cut)

    def half_lanes(k, d):
        return pl.ds(pl.multiple_of(k * cut + d * half_cut, half_cut), half_cut)

    def remote(src, dst, s_sem, r_sem, to):
        return pltpu.make_async_remote_copy(
            src_ref=src, dst_ref=dst, send_sem=s_sem, recv_sem=r_sem, device_id=to, device_id_type=MESH)

    load_v = pltpu.make_async_copy(wv_hbm.at[0], wv, w_sem.at[0])
    load_o = pltpu.make_async_copy(wo_hbm.at[0], wo, w_sem.at[1])

    barrier = pltpu.get_barrier_semaphore()

    def greet(to):
        pl.semaphore_signal(barrier, inc=1, device_id=to, device_id_type=MESH)

    greet(side[RIGHT])
    greet(side[LEFT])
    greet(across)

    @pl.when(p > 0)
    def _():
        greet((p - 1, w, h))
        greet((p - 1, w_from, h))

    @pl.when(odd == 1)
    def _():
        greet((p, w_prev, h))

    @pl.when(p > 0)
    def _():
        load_v.start()
        load_o.start()

    for k in range(n_pipe):
        @pl.when(p == k)
        def _():
            pl.semaphore_wait(barrier, 3 + 2 * (k < n_pipe - 1) + k % 2)

    def span(c):
        a, r0, nr = CHUNKS[c]
        return a * half + r0 * half_cols, nr * half_cols

    def direct_sum(c):
        return c == 0

    def direct_gather(c):
        return c == COUNT - 1

    def normalize(a):
        x = xin[a].reshape(half, width).astype(F32)
        inverse = lax.rsqrt(jnp.sum(x * x, axis=1, keepdims=True) * (1.0 / width) + EPSILON)
        u = (x * inverse).astype(BF16)
        mine = xin[a, :, :, lanes(h)].reshape(half, cut).astype(F32)
        ubuf[a * half:(a + 1) * half, :] = (mine * inverse).astype(BF16)
        vbuf[a * half:(a + 1) * half, :] = jnp.dot(u, wv[...], preferred_element_type=F32).astype(BF16)

    @pl.when(p == 0)
    def _():
        def rows_of(k):
            return pl.ds(k * my_rows, my_rows)

        def spread(a, d):
            return remote(
                stream.at[:, pl.ds(a * half_cols, half_cols)], xin.at[a, rows_of(h)],
                ag_s.at[d, a], ag_r.at[d, a], side[d])

        def relay(a, d):
            row = (left if d == RIGHT else right) * my_rows + d
            part = xin.at[a, pl.ds(row, 1)]
            return remote(part, part, rl_s.at[d, a], rl_r.at[d, a], side[d])

        own = [
            pltpu.make_async_copy(
                stream.at[:, pl.ds(a * half_cols, half_cols)], xin.at[a, rows_of(h)], own_sem.at[a])
            for a in range(2)
        ]
        for a in range(2):
            for d in (RIGHT, LEFT):
                spread(a, d).start()
            own[a].start()
        load_v.start()
        load_o.start()
        for a in range(2):
            for d in (RIGHT, LEFT):
                spread(a, d).wait_recv()
                relay(a, d).start()
        load_v.wait()
        for a in range(2):
            own[a].wait()
            for d in (RIGHT, LEFT):
                relay(a, d).wait_recv()
            normalize(a)
        for a in range(2):
            for d in (RIGHT, LEFT):
                spread(a, d).wait_send()
                relay(a, d).wait_send()

    def hand_on(c):
        a, r0, nr = CHUNKS[c]
        to = (p + 1, w_to if a == 0 else w, h)
        return remote(
            xnew.at[a, pl.ds(r0, nr)], xin.at[a, pl.ds(r0, nr), :, lanes(h)],
            pp_s.at[c], pp_r.at[c], to)

    @pl.when(p > 0)
    def _():
        def spread(c, d):
            a, r0, nr = CHUNKS[c]
            part = xin.at[a, pl.ds(r0, nr), :, lanes(h)]
            return remote(part, part, ag_s.at[d, c], ag_r.at[d, c], side[d])

        def relays(c):
            a, r0, nr = CHUNKS[c]
            if direct_gather(c):
                part = xin.at[a, pl.ds(r0, nr), :, lanes(h)]
                return [remote(part, part, rl_s.at[0, c], rl_r.at[0, c], across)]
            made = []
            for d in (RIGHT, LEFT):
                part = xin.at[a, pl.ds(r0, nr), :, half_lanes(left if d == RIGHT else right, d)]
                made.append(remote(part, part, rl_s.at[d, c], rl_r.at[d, c], side[d]))
            return made

        load_v.wait()
        for i in range(COUNT + 2):
            if i < COUNT:
                hand_on(i).wait_recv()
                for d in (RIGHT, LEFT):
                    spread(i, d).start()
                if direct_gather(i):
                    relays(i)[0].start()
            if 1 <= i <= COUNT:
                for d in (RIGHT, LEFT):
                    spread(i - 1, d).wait_recv()
                    if not direct_gather(i - 1):
                        relays(i - 1)[d].start()
            if i >= 2:
                for copy in relays(i - 2):
                    copy.wait_recv()
                if i - 2 == FIRST_OF_1 - 1:
                    normalize(0)
        normalize(1)
        for c in range(COUNT):
            for d in (RIGHT, LEFT):
                spread(c, d).wait_send()
            for copy in relays(c):
                copy.wait_send()

    load_o.wait()
    inv_root = 1.0 / math.sqrt(HEAD_DIM)

    def attend(a):
        for j in range(heads):
            col = slice(j * HEAD_DIM, (j + 1) * HEAD_DIM)
            gain = scale[:, pl.ds(pl.multiple_of(h * cut + j * HEAD_DIM, HEAD_DIM), HEAD_DIM)]
            q = (ubuf[a * half:(a + 1) * half, col].astype(F32) * gain).astype(BF16)
            s = lax.dot_general(q, ubuf[:, col], (((1,), (1,)), ((), ())), preferred_element_type=F32) * inv_root
            e = jnp.exp(s - jnp.max(s, axis=1, keepdims=True))
            prob = (e / jnp.sum(e, axis=1, keepdims=True)).astype(BF16)
            obuf[a, :, col] = jnp.dot(prob, vbuf[:, col], preferred_element_type=F32).astype(BF16)

    def project(a, k):
        return jnp.dot(obuf[a], wo[:, lanes(k)], preferred_element_type=F32)

    def far_shares(c):
        t0, n = span(c)
        if direct_sum(c):
            return [remote(g2.at[pl.ds(t0, n)], rfar, r2_s.at[0, c], r2_r.at[0, c], across)]
        return [
            remote(g2.at[pl.ds(t0, n), pl.ds(d * half_cut, half_cut)], r2.at[d, pl.ds(t0, n)],
                   r2_s.at[d, c], r2_r.at[d, c], side[d])
            for d in (RIGHT, LEFT)
        ]

    def near_share(c, d):
        t0, n = span(c)
        return remote(gsend.at[d, pl.ds(t0, n)], grecv.at[d, pl.ds(t0, n)], rs_s.at[d, c], rs_r.at[d, c], side[d])

    def cols_of(a):
        return pl.ds(a * half_cols, half_cols)

    def keep(c):
        a, r0, nr = CHUNKS[c]
        return pltpu.make_async_copy(
            xnew.at[a, pl.ds(r0, nr)], out.at[0, pl.ds(r0, nr), cols_of(a)], out_sem.at[c])

    def keep_next(c):
        a, r0, nr = CHUNKS[c]
        return remote(
            xnew.at[a, pl.ds(r0, nr)], out.at[0, pl.ds(r0, nr), cols_of(a)],
            os_s.at[c], os_r.at[c], (p, w_next, h))

    def near(c):
        t0, n = span(c)
        cells = slice(t0, t0 + n)
        if not direct_sum(c):
            for copy in far_shares(c):
                copy.wait_recv()
        for d in (RIGHT, LEFT):
            if direct_sum(c):
                gsend[d, cells] = gside[d, cells].astype(BF16)
            else:
                mid = slice(d * half_cut, (d + 1) * half_cut)
                rest = slice((1 - d) * half_cut, (2 - d) * half_cut)
                gsend[d, cells, mid] = (gside[d, cells, mid] + r2[d, cells].astype(F32)).astype(BF16)
                gsend[d, cells, rest] = gside[d, cells, rest].astype(BF16)
            near_share(c, d).start()

    def finish(c):
        a, r0, nr = CHUNKS[c]
        t0, n = span(c)
        cells = slice(t0, t0 + n)
        total = xin[a, r0:r0 + nr, :, lanes(h)].reshape(n, cut).astype(F32) + gown[cells]
        for d in (RIGHT, LEFT):
            near_share(c, d).wait_recv()
            total = total + grecv[d, cells].astype(F32)
        if direct_sum(c):
            far_shares(c)[0].wait_recv()
            total = total + rfar[...].astype(F32)
        xnew[a, r0:r0 + nr] = total.astype(BF16).reshape(nr, half_cols, cut)

        @pl.when(p < n_pipe - 1)
        def _():
            hand_on(c).start()

        if a == 1:
            keep(c).start()
        else:
            @pl.when(odd == 0)
            def _():
                keep(c).start()

            @pl.when(odd == 1)
            def _():
                keep_next(c).start()

    def send_far(c):
        for copy in far_shares(c):
            copy.start()

    for a in range(2):
        cells = slice(a * half, (a + 1) * half)
        attend(a)
        g2[cells] = project(a, far).astype(BF16)
        if a == 0:
            for c in range(FIRST_OF_1):
                send_far(c)
        gside[RIGHT, cells] = project(a, right)
        gside[LEFT, cells] = project(a, left)
        if a == 0:
            near(0)
        gown[cells] = project(a, h)

    for i in range(1, COUNT + 2):
        if i < COUNT:
            near(i)
        ahead = i + FIRST_OF_1 - 1
        if ahead < COUNT:
            send_far(ahead)
        if i == 1:
            finish(0)
        if i >= 3:
            finish(i - 2)

    for c in range(COUNT):
        for d in (RIGHT, LEFT):
            near_share(c, d).wait_send()
        for copy in far_shares(c):
            copy.wait_send()

        @pl.when(p < n_pipe - 1)
        def _():
            hand_on(c).wait_send()

        if CHUNKS[c][0] == 1:
            keep(c).wait()
        else:
            @pl.when(odd == 0)
            def _():
                keep(c).wait()

            @pl.when(odd == 1)
            def _():
                keep_next(c).wait_send()
                keep_next(c).wait_recv()


def solution(mesh):
    sizes = tuple(mesh.shape[name] for name in ("pipe", "win", "head"))

    def per_device(stream, score_scale, value_weight, out_weight):
        my_rows, cols, width = stream.shape
        rows, half_cols, cut = my_rows * sizes[2], cols // 2, width // sizes[2]
        cells = rows * cols
        anywhere = pl.BlockSpec(memory_space=pl.ANY)
        dma = pltpu.SemaphoreType.DMA
        return pl.pallas_call(
            functools.partial(kernel, sizes),
            out_shape=jax.ShapeDtypeStruct((1, rows, cols, cut), BF16),
            in_specs=[anywhere, pl.BlockSpec(memory_space=pltpu.VMEM), anywhere, anywhere],
            out_specs=anywhere,
            scratch_shapes=[
                pltpu.VMEM((2, rows, half_cols, width), BF16),
                pltpu.VMEM((width, cut), BF16),
                pltpu.VMEM((cut, width), BF16),
                pltpu.VMEM((cells, cut), BF16),
                pltpu.VMEM((cells, cut), BF16),
                pltpu.VMEM((2, cells // 2, cut), BF16),
                pltpu.VMEM((cells, cut), BF16),
                pltpu.VMEM((2, cells, cut // 2), BF16),
                pltpu.VMEM((CHUNKS[0][2] * half_cols, cut), BF16),
                pltpu.VMEM((cells, cut), F32),
                pltpu.VMEM((2, cells, cut), F32),
                pltpu.VMEM((2, cells, cut), BF16),
                pltpu.VMEM((2, cells, cut), BF16),
                pltpu.VMEM((2, rows, half_cols, cut), BF16),
                dma((2,)), dma((2,)),
                dma((2, COUNT)), dma((2, COUNT)),
                dma((2, COUNT)), dma((2, COUNT)),
                dma((2, COUNT)), dma((2, COUNT)),
                dma((2, COUNT)), dma((2, COUNT)),
                dma((COUNT,)), dma((COUNT,)),
                dma((COUNT,)), dma((COUNT,)),
                dma((COUNT,)),
            ],
            compiler_params=pltpu.CompilerParams(collective_id=0, has_side_effects=True),
        )(stream, score_scale, value_weight, out_weight)

    return jax.shard_map(
        per_device,
        mesh=mesh,
        in_specs=(P("head", "win", None), P("pipe", None), P("pipe", None, "head"), P("pipe", "head", None)),
        out_specs=P("pipe", None, "win", "head"),
        check_vma=False,
    )
```

time: 175 us -> 131 us (0.75)
  Pallas kernels: 174 us -> 130 us
    pallas_call x1, Pallas kernels: 174 us -> 130 us  [per_device(): pl.pallas_call(functools.partial(kernel, sizes), out_shape=jax.ShapeDtype...]
where the time goes in v3:
time: 131 us
  Pallas kernels  130 us (99%)
  local copies, waits for them, and re-layouts  1.67 us (1%)
    pallas_call x1, Pallas kernels, per_device(): pl.pallas_call(functools.partial(kernel, sizes), out_shape=jax.ShapeDtype...  130 us

profile of v3, /device:TPU:50, one launch (start us, length us, event | category | flops | bytes accessed | tf_op | source)
XLA Modules:
  0.0 131.3 jit_solution(7279387639565216004)
XLA Ops:
  0.0 129.6 %shard_map.46 = bf16[1,8,32,512]{3,2,1,0:T(8,128)(2,1)} custom-call(bf16[2,32,2048]{2,1,0:T(8,128)(2,1)} %stream.1, f32[1,2048]{1,0:T(1,128)} %scale.1, bf16[1,2048,512]{2,1,0:T(8,128)(2,1)} %wv_hbm.1, bf16[1,512,2048]{2,1,0:T(8,128)(2,1)} %wo_hbm.1), custom_call_target="tpu_custom_call" | custom-call | tf_op jit(solution)/shard_map/pallas_call | solution.py:341
  129.6 1.7 %copy.6 = bf16[1,8,32,512]{3,2,1,0:T(8,128)(2,1)} copy(bf16[1,8,32,512]{3,2,1,0:T(8,128)(2,1)} %shard_map.46) | data formatting | bytes 524288

commit v4 on v3

v4 whole, which is shorter than its diff:
```python
import functools
import math

import jax
import jax.numpy as jnp
from jax import lax
from jax.experimental import pallas as pl
from jax.experimental.pallas import tpu as pltpu
from jax.sharding import PartitionSpec as P

MESH = pl.DeviceIdType.MESH
HEAD_DIM = 128
EPSILON = 1e-06
BF16, F32 = jnp.bfloat16, jnp.float32

CHUNKS = ((0, 0, 2), (0, 2, 2), (0, 4, 2), (0, 6, 2), (1, 0, 2), (1, 2, 2), (1, 4, 2), (1, 6, 2))
COUNT = len(CHUNKS)
FIRST_OF_1 = next(c for c in range(COUNT) if CHUNKS[c][0] == 1)
HALVES = (range(FIRST_OF_1), range(FIRST_OF_1, COUNT))
PEERS = (2, 1, 3)


def kernel(
    sizes, stream, scale, wv_hbm, wo_hbm, out,
    xin, wv, wo, ubuf, vbuf, obuf, gown, gsend, grecv, xnew,
    w_sem, own_sem, ag_s, ag_r, rs_s, rs_r, pp_s, pp_r, os_s, os_r, out_sem,
):
    n_pipe, n_win, n_head = sizes
    rows, half_cols, width = xin.shape[1:]
    cut = width // n_head
    heads = cut // HEAD_DIM
    half = rows * half_cols
    my_rows = stream.shape[0]
    p, w, h = lax.axis_index("pipe"), lax.axis_index("win"), lax.axis_index("head")
    odd = lax.rem(p, 2)
    peer = [lax.rem(h + k, n_head) for k in PEERS]
    w_next, w_prev = lax.rem(w + 1, n_win), lax.rem(w + n_win - 1, n_win)
    w_to = lax.rem(w + n_win - 1 + 2 * odd, n_win)
    w_from = lax.rem(w + n_win - 1 + 2 * odd, n_win)
    def lanes(k):
        return pl.ds(pl.multiple_of(k * cut, cut), cut)

    def remote(src, dst, s_sem, r_sem, to):
        return pltpu.make_async_remote_copy(
            src_ref=src, dst_ref=dst, send_sem=s_sem, recv_sem=r_sem, device_id=to, device_id_type=MESH)

    load_v = pltpu.make_async_copy(wv_hbm.at[0], wv, w_sem.at[0])
    load_o = pltpu.make_async_copy(wo_hbm.at[0], wo, w_sem.at[1])

    barrier = pltpu.get_barrier_semaphore()

    def greet(to):
        pl.semaphore_signal(barrier, inc=1, device_id=to, device_id_type=MESH)

    for k in peer:
        greet((p, w, k))

    @pl.when(p == 0)
    def _():
        greet((1, w, peer[0]))

    @pl.when(p > 0)
    def _():
        greet((p - 1, w, h))
        greet((p - 1, w_from, h))

    @pl.when(odd == 1)
    def _():
        greet((p, w_prev, h))

    load_v.start()
    load_o.start()

    for k in range(n_pipe):
        @pl.when(p == k)
        def _():
            pl.semaphore_wait(barrier, 3 + 2 * (k < n_pipe - 1) + k % 2 + (k == 1))

    def span(c):
        a, r0, nr = CHUNKS[c]
        return a * half + r0 * half_cols, nr * half_cols

    def normalize(a):
        x = xin[a].reshape(half, width).astype(F32)
        inverse = lax.rsqrt(jnp.sum(x * x, axis=1, keepdims=True) * (1.0 / width) + EPSILON)
        u = (x * inverse).astype(BF16)
        mine = xin[a, :, :, lanes(h)].reshape(half, cut).astype(F32)
        ubuf[a * half:(a + 1) * half, :] = (mine * inverse).astype(BF16)
        vbuf[a * half:(a + 1) * half, :] = jnp.dot(u, wv[...], preferred_element_type=F32).astype(BF16)

    def first_rows(a, d):
        cols = pl.ds(a * half_cols, half_cols)
        return remote(
            stream.at[:, cols], xin.at[a, pl.ds(h * my_rows, my_rows)],
            ag_s.at[d, a], ag_r.at[d, a], (0, w, peer[d]))

    @pl.when(p == 0)
    def _():
        own = [
            pltpu.make_async_copy(
                stream.at[:, pl.ds(a * half_cols, half_cols)], xin.at[a, pl.ds(h * my_rows, my_rows)], own_sem.at[a])
            for a in range(2)
        ]
        for a in range(2):
            for d in (1, 2):
                first_rows(a, d).start()
            own[a].start()
        load_v.wait()
        for a in range(2):
            own[a].wait()
            for d in range(3):
                first_rows(a, d).wait_recv()
            normalize(a)
        for a in range(2):
            for d in (1, 2):
                first_rows(a, d).wait_send()

    @pl.when(p == 1)
    def _():
        for a in range(2):
            first_rows(a, 0).start()
        for a in range(2):
            first_rows(a, 0).wait_send()

    def hand_on(c):
        a, r0, nr = CHUNKS[c]
        to = (p + 1, w_to if a == 0 else w, h)
        return remote(
            xnew.at[a, pl.ds(r0, nr)], xin.at[a, pl.ds(r0, nr), :, lanes(h)],
            pp_s.at[c], pp_r.at[c], to)

    @pl.when(p > 0)
    def _():
        def spread(c, d):
            a, r0, nr = CHUNKS[c]
            part = xin.at[a, pl.ds(r0, nr), :, lanes(h)]
            return remote(part, part, ag_s.at[d, c], ag_r.at[d, c], (p, w, peer[d]))

        load_v.wait()
        for c in range(COUNT):
            hand_on(c).wait_recv()
            for d in range(3):
                spread(c, d).start()
        for a in range(2):
            for c in HALVES[a]:
                for d in range(3):
                    spread(c, d).wait_recv()
            normalize(a)
        for c in range(COUNT):
            for d in range(3):
                spread(c, d).wait_send()

    load_o.wait()
    inv_root = 1.0 / math.sqrt(HEAD_DIM)

    def attend(a):
        for j in range(heads):
            col = slice(j * HEAD_DIM, (j + 1) * HEAD_DIM)
            gain = scale[:, pl.ds(pl.multiple_of(h * cut + j * HEAD_DIM, HEAD_DIM), HEAD_DIM)]
            q = (ubuf[a * half:(a + 1) * half, col].astype(F32) * gain).astype(BF16)
            s = lax.dot_general(q, ubuf[:, col], (((1,), (1,)), ((), ())), preferred_element_type=F32) * inv_root
            e = jnp.exp(s - jnp.max(s, axis=1, keepdims=True))
            prob = (e / jnp.sum(e, axis=1, keepdims=True)).astype(BF16)
            obuf[a, :, col] = jnp.dot(prob, vbuf[:, col], preferred_element_type=F32).astype(BF16)

    def project(a, k):
        return jnp.dot(obuf[a], wo[:, lanes(k)], preferred_element_type=F32)

    def share(c, d):
        t0, n = span(c)
        return remote(
            gsend.at[d, pl.ds(t0, n)], grecv.at[d, pl.ds(t0, n)], rs_s.at[d, c], rs_r.at[d, c], (p, w, peer[d]))

    def cols_of(a):
        return pl.ds(a * half_cols, half_cols)

    def keep(c):
        a, r0, nr = CHUNKS[c]
        return pltpu.make_async_copy(
            xnew.at[a, pl.ds(r0, nr)], out.at[0, pl.ds(r0, nr), cols_of(a)], out_sem.at[c])

    def keep_next(c):
        a, r0, nr = CHUNKS[c]
        return remote(
            xnew.at[a, pl.ds(r0, nr)], out.at[0, pl.ds(r0, nr), cols_of(a)],
            os_s.at[c], os_r.at[c], (p, w_next, h))

    def finish(c):
        a, r0, nr = CHUNKS[c]
        t0, n = span(c)
        cells = slice(t0, t0 + n)
        total = xin[a, r0:r0 + nr, :, lanes(h)].reshape(n, cut).astype(F32) + gown[cells]
        for d in range(3):
            share(c, d).wait_recv()
            total = total + grecv[d, cells].astype(F32)
        xnew[a, r0:r0 + nr] = total.astype(BF16).reshape(nr, half_cols, cut)

        @pl.when(p < n_pipe - 1)
        def _():
            hand_on(c).start()

        if a == 1:
            keep(c).start()
        else:
            @pl.when(odd == 0)
            def _():
                keep(c).start()

            @pl.when(odd == 1)
            def _():
                keep_next(c).start()

    for a in range(2):
        cells = slice(a * half, (a + 1) * half)
        attend(a)
        for d in range(3):
            gsend[d, cells] = project(a, peer[d]).astype(BF16)
        for c in HALVES[a]:
            for d in range(3):
                share(c, d).start()
        gown[cells] = project(a, h)

    for c in range(COUNT):
        finish(c)

    for c in range(COUNT):
        for d in range(3):
            share(c, d).wait_send()

        @pl.when(p < n_pipe - 1)
        def _():
            hand_on(c).wait_send()

        if CHUNKS[c][0] == 1:
            keep(c).wait()
        else:
            @pl.when(odd == 0)
            def _():
                keep(c).wait()

            @pl.when(odd == 1)
            def _():
                keep_next(c).wait_send()
                keep_next(c).wait_recv()


def solution(mesh):
    sizes = tuple(mesh.shape[name] for name in ("pipe", "win", "head"))

    def per_device(stream, score_scale, value_weight, out_weight):
        my_rows, cols, width = stream.shape
        rows, half_cols, cut = my_rows * sizes[2], cols // 2, width // sizes[2]
        cells = rows * cols
        anywhere = pl.BlockSpec(memory_space=pl.ANY)
        dma = pltpu.SemaphoreType.DMA
        return pl.pallas_call(
            functools.partial(kernel, sizes),
            out_shape=jax.ShapeDtypeStruct((1, rows, cols, cut), BF16),
            in_specs=[anywhere, pl.BlockSpec(memory_space=pltpu.VMEM), anywhere, anywhere],
            out_specs=anywhere,
            scratch_shapes=[
                pltpu.VMEM((2, rows, half_cols, width), BF16),
                pltpu.VMEM((width, cut), BF16),
                pltpu.VMEM((cut, width), BF16),
                pltpu.VMEM((cells, cut), BF16),
                pltpu.VMEM((cells, cut), BF16),
                pltpu.VMEM((2, cells // 2, cut), BF16),
                pltpu.VMEM((cells, cut), F32),
                pltpu.VMEM((3, cells, cut), BF16),
                pltpu.VMEM((3, cells, cut), BF16),
                pltpu.VMEM((2, rows, half_cols, cut), BF16),
                dma((2,)), dma((2,)),
                dma((3, COUNT)), dma((3, COUNT)),
                dma((3, COUNT)), dma((3, COUNT)),
                dma((COUNT,)), dma((COUNT,)),
                dma((COUNT,)), dma((COUNT,)),
                dma((COUNT,)),
            ],
            compiler_params=pltpu.CompilerParams(collective_id=0, has_side_effects=True),
        )(stream, score_scale, value_weight, out_weight)

    return jax.shard_map(
        per_device,
        mesh=mesh,
        in_specs=(P("head", "win", None), P("pipe", None), P("pipe", None, "head"), P("pipe", "head", None)),
        out_specs=P("pipe", None, "win", "head"),
        check_vma=False,
    )
```

time: 131 us -> 113 us (0.86)
  the two profiles are of different devices: /device:TPU:50 before, /device:TPU:54 now
where the time goes in v4:
time: 113 us
  Pallas kernels  111 us (98%)
  local copies, waits for them, and re-layouts  1.67 us (1%)
    pallas_call x1, Pallas kernels, per_device(): pl.pallas_call(functools.partial(kernel, sizes), out_shape=jax.ShapeDtype...  111 us

profile of v4, /device:TPU:54, one launch (start us, length us, event | category | flops | bytes accessed | tf_op | source)
XLA Modules:
  0.0 113.0 jit_solution(6433934878850298783)
XLA Ops:
  0.0 111.3 %shard_map.46 = bf16[1,8,32,512]{3,2,1,0:T(8,128)(2,1)} custom-call(bf16[2,32,2048]{2,1,0:T(8,128)(2,1)} %stream.1, f32[1,2048]{1,0:T(1,128)} %scale.1, bf16[1,2048,512]{2,1,0:T(8,128)(2,1)} %wv_hbm.1, bf16[1,512,2048]{2,1,0:T(8,128)(2,1)} %wo_hbm.1), custom_call_target="tpu_custom_call" | custom-call | tf_op jit(solution)/shard_map/pallas_call | solution.py:256
  111.3 1.7 %copy.6 = bf16[1,8,32,512]{3,2,1,0:T(8,128)(2,1)} copy(bf16[1,8,32,512]{3,2,1,0:T(8,128)(2,1)} %shard_map.46) | data formatting | bytes 524288

commit v5 on v4

--- a/solution.py
+++ b/solution.py
@@ -13,7 +13,7 @@
 EPSILON = 1e-06
 BF16, F32 = jnp.bfloat16, jnp.float32
 
-CHUNKS = ((0, 0, 2), (0, 2, 2), (0, 4, 2), (0, 6, 2), (1, 0, 2), (1, 2, 2), (1, 4, 2), (1, 6, 2))
+CHUNKS = tuple((a, r, 1) for a in range(2) for r in range(8))
 COUNT = len(CHUNKS)
 FIRST_OF_1 = next(c for c in range(COUNT) if CHUNKS[c][0] == 1)
 HALVES = (range(FIRST_OF_1), range(FIRST_OF_1, COUNT))
@@ -22,8 +22,8 @@
 
 def kernel(
     sizes, stream, scale, wv_hbm, wo_hbm, out,
-    xin, wv, wo, ubuf, vbuf, obuf, gown, gsend, grecv, xnew,
-    w_sem, own_sem, ag_s, ag_r, rs_s, rs_r, pp_s, pp_r, os_s, os_r, out_sem,
+    xin, wv, wo, ubuf, vbuf, obuf, gown, gsend, grecv, xnew, via,
+    w_sem, own_sem, ag_s, ag_r, v1_s, v1_r, v2_s, v2_r, rs_s, rs_r, pp_s, pp_r, os_s, os_r, out_sem,
 ):
     n_pipe, n_win, n_head = sizes
     rows, half_cols, width = xin.shape[1:]
@@ -57,7 +57,8 @@
 
     @pl.when(p == 0)
     def _():
-        greet((1, w, peer[0]))
+        greet((1, w, h))
+        greet((3, w, h))
 
     @pl.when(p > 0)
     def _():
@@ -74,7 +75,7 @@
     for k in range(n_pipe):
         @pl.when(p == k)
         def _():
-            pl.semaphore_wait(barrier, 3 + 2 * (k < n_pipe - 1) + k % 2 + (k == 1))
+            pl.semaphore_wait(barrier, 3 + 2 * (k < n_pipe - 1) + 2 * (k % 2))
 
     def span(c):
         a, r0, nr = CHUNKS[c]
@@ -88,39 +89,54 @@
         ubuf[a * half:(a + 1) * half, :] = (mine * inverse).astype(BF16)
         vbuf[a * half:(a + 1) * half, :] = jnp.dot(u, wv[...], preferred_element_type=F32).astype(BF16)
 
+    def cols_of(a):
+        return pl.ds(a * half_cols, half_cols)
+
     def first_rows(a, d):
-        cols = pl.ds(a * half_cols, half_cols)
         return remote(
-            stream.at[:, cols], xin.at[a, pl.ds(h * my_rows, my_rows)],
-            ag_s.at[d, a], ag_r.at[d, a], (0, w, peer[d]))
+            stream.at[:, cols_of(a)], xin.at[a, pl.ds(h * my_rows, my_rows)],
+            ag_s.at[d, a], ag_r.at[d, a], (p, w, peer[d]))
+
+    def cross(row):
+        return remote(stream.at[pl.ds(row, 1), cols_of(1)], via, v1_s.at[0], v1_r.at[0], (p, w, peer[0]))
+
+    def drop(row):
+        return remote(via, xin.at[1, pl.ds(peer[0] * my_rows + row, 1)], v2_s.at[0], v2_r.at[row], (0, w, h))
+
+    FIRST = ((0, (0, 1, 2)), (1, (1, 2)))
 
     @pl.when(p == 0)
     def _():
         own = [
             pltpu.make_async_copy(
-                stream.at[:, pl.ds(a * half_cols, half_cols)], xin.at[a, pl.ds(h * my_rows, my_rows)], own_sem.at[a])
+                stream.at[:, cols_of(a)], xin.at[a, pl.ds(h * my_rows, my_rows)], own_sem.at[a])
             for a in range(2)
         ]
-        for a in range(2):
-            for d in (1, 2):
+        for a, ways in FIRST:
+            for d in ways:
                 first_rows(a, d).start()
             own[a].start()
         load_v.wait()
-        for a in range(2):
+        for a, ways in FIRST:
             own[a].wait()
-            for d in range(3):
+            for d in ways:
                 first_rows(a, d).wait_recv()
+            if a == 1:
+                for row in range(2):
+                    drop(row).wait_recv()
             normalize(a)
-        for a in range(2):
-            for d in (1, 2):
+        for a, ways in FIRST:
+            for d in ways:
                 first_rows(a, d).wait_send()
 
-    @pl.when(p == 1)
-    def _():
-        for a in range(2):
-            first_rows(a, 0).start()
-        for a in range(2):
-            first_rows(a, 0).wait_send()
+    for row in range(2):
+        @pl.when(p == 2 * row + 1)
+        def _():
+            cross(row).start()
+            cross(row).wait_recv()
+            drop(row).start()
+            cross(row).wait_send()
+            drop(row).wait_send()
 
     def hand_on(c):
         a, r0, nr = CHUNKS[c]
@@ -170,9 +186,6 @@
         t0, n = span(c)
         return remote(
             gsend.at[d, pl.ds(t0, n)], grecv.at[d, pl.ds(t0, n)], rs_s.at[d, c], rs_r.at[d, c], (p, w, peer[d]))
-
-    def cols_of(a):
-        return pl.ds(a * half_cols, half_cols)
 
     def keep(c):
         a, r0, nr = CHUNKS[c]
@@ -269,8 +282,10 @@
                 pltpu.VMEM((3, cells, cut), BF16),
                 pltpu.VMEM((3, cells, cut), BF16),
                 pltpu.VMEM((2, rows, half_cols, cut), BF16),
+                pltpu.VMEM((1, half_cols, width), BF16),
                 dma((2,)), dma((2,)),
                 dma((3, COUNT)), dma((3, COUNT)),
+                dma((1,)), dma((1,)), dma((1,)), dma((2,)),
                 dma((3, COUNT)), dma((3, COUNT)),
                 dma((COUNT,)), dma((COUNT,)),
                 dma((COUNT,)), dma((COUNT,)),

time: 113 us -> 110 us (0.973)
  the two profiles are of different devices: /device:TPU:54 before, /device:TPU:48 now
where the time goes in v5:
time: 110 us
  Pallas kernels  108 us (98%)
  local copies, waits for them, and re-layouts  1.67 us (2%)
    pallas_call x1, Pallas kernels, per_device(): pl.pallas_call(functools.partial(kernel, sizes), out_shape=jax.ShapeDtype...  108 us

profile of v5, /device:TPU:48, one launch (start us, length us, event | category | flops | bytes accessed | tf_op | source)
XLA Modules:
  0.0 109.8 jit_solution(16966268680396502674)
XLA Ops:
  0.0 108.1 %shard_map.46 = bf16[1,8,32,512]{3,2,1,0:T(8,128)(2,1)} custom-call(bf16[2,32,2048]{2,1,0:T(8,128)(2,1)} %stream.1, f32[1,2048]{1,0:T(1,128)} %scale.1, bf16[1,2048,512]{2,1,0:T(8,128)(2,1)} %wv_hbm.1, bf16[1,512,2048]{2,1,0:T(8,128)(2,1)} %wo_hbm.1), custom_call_target="tpu_custom_call" | custom-call | tf_op jit(solution)/shard_map/pallas_call | solution.py:269
  108.1 1.7 %copy.6 = bf16[1,8,32,512]{3,2,1,0:T(8,128)(2,1)} copy(bf16[1,8,32,512]{3,2,1,0:T(8,128)(2,1)} %shard_map.46) | data formatting | bytes 524288

commit v6 on v5

--- a/solution.py
+++ b/solution.py
@@ -18,12 +18,13 @@
 FIRST_OF_1 = next(c for c in range(COUNT) if CHUNKS[c][0] == 1)
 HALVES = (range(FIRST_OF_1), range(FIRST_OF_1, COUNT))
 PEERS = (2, 1, 3)
+DETOUR = tuple(range(7))
 
 
 def kernel(
     sizes, stream, scale, wv_hbm, wo_hbm, out,
-    xin, wv, wo, ubuf, vbuf, obuf, gown, gsend, grecv, xnew, via,
-    w_sem, own_sem, ag_s, ag_r, v1_s, v1_r, v2_s, v2_r, rs_s, rs_r, pp_s, pp_r, os_s, os_r, out_sem,
+    xin, wv, wo, ubuf, vbuf, obuf, gown, gsend, grecv, xnew, via, stop,
+    w_sem, own_sem, ag_s, ag_r, v1_s, v1_r, v2_s, v2_r, m1_s, m1_r, m2_s, rs_s, rs_r, pp_s, pp_r, os_s, os_r, out_sem,
 ):
     n_pipe, n_win, n_head = sizes
     rows, half_cols, width = xin.shape[1:]
@@ -35,8 +36,8 @@
     odd = lax.rem(p, 2)
     peer = [lax.rem(h + k, n_head) for k in PEERS]
     w_next, w_prev = lax.rem(w + 1, n_win), lax.rem(w + n_win - 1, n_win)
-    w_to = lax.rem(w + n_win - 1 + 2 * odd, n_win)
-    w_from = lax.rem(w + n_win - 1 + 2 * odd, n_win)
+    w_to = lax.rem(w + n_win + 1 - 2 * odd, n_win)
+    w_from = lax.rem(w + n_win + 1 - 2 * odd, n_win)
     def lanes(k):
         return pl.ds(pl.multiple_of(k * cut, cut), cut)
 
@@ -55,6 +56,10 @@
     for k in peer:
         greet((p, w, k))
 
+    @pl.when(p == n_pipe - 2)
+    def _():
+        greet((p + 1, w, peer[0]))
+
     @pl.when(p == 0)
     def _():
         greet((1, w, h))
@@ -67,7 +72,7 @@
 
     @pl.when(odd == 1)
     def _():
-        greet((p, w_prev, h))
+        greet((p, w_next, h))
 
     load_v.start()
     load_o.start()
@@ -75,7 +80,7 @@
     for k in range(n_pipe):
         @pl.when(p == k)
         def _():
-            pl.semaphore_wait(barrier, 3 + 2 * (k < n_pipe - 1) + 2 * (k % 2))
+            pl.semaphore_wait(barrier, 3 + 2 * (k < n_pipe - 1) + 2 * (k % 2) + (k == n_pipe - 1))
 
     def span(c):
         a, r0, nr = CHUNKS[c]
@@ -90,7 +95,7 @@
         vbuf[a * half:(a + 1) * half, :] = jnp.dot(u, wv[...], preferred_element_type=F32).astype(BF16)
 
     def cols_of(a):
-        return pl.ds(a * half_cols, half_cols)
+        return pl.ds((1 - a) * half_cols, half_cols)
 
     def first_rows(a, d):
         return remote(
@@ -187,6 +192,16 @@
         return remote(
             gsend.at[d, pl.ds(t0, n)], grecv.at[d, pl.ds(t0, n)], rs_s.at[d, c], rs_r.at[d, c], (p, w, peer[d]))
 
+    def detour(c):
+        t0, n = span(c)
+        return remote(
+            gsend.at[0, pl.ds(t0, n)], stop.at[pl.ds(t0, n)], m1_s.at[c], m1_r.at[c], (n_pipe - 2, w, peer[0]))
+
+    def rejoin(c):
+        t0, n = span(c)
+        return remote(
+            stop.at[pl.ds(t0, n)], grecv.at[0, pl.ds(t0, n)], m2_s.at[c], rs_r.at[0, c], (n_pipe - 1, w, h))
+
     def keep(c):
         a, r0, nr = CHUNKS[c]
         return pltpu.make_async_copy(
@@ -196,7 +211,7 @@
         a, r0, nr = CHUNKS[c]
         return remote(
             xnew.at[a, pl.ds(r0, nr)], out.at[0, pl.ds(r0, nr), cols_of(a)],
-            os_s.at[c], os_r.at[c], (p, w_next, h))
+            os_s.at[c], os_r.at[c], (p, w_prev, h))
 
     def finish(c):
         a, r0, nr = CHUNKS[c]
@@ -229,7 +244,15 @@
         for d in range(3):
             gsend[d, cells] = project(a, peer[d]).astype(BF16)
         for c in HALVES[a]:
-            for d in range(3):
+            if c in DETOUR:
+                @pl.when(p < n_pipe - 1)
+                def _():
+                    share(c, 0).start()
+
+                @pl.when(p == n_pipe - 1)
+                def _():
+                    detour(c).start()
+            for d in range(1 if c in DETOUR else 0, 3):
                 share(c, d).start()
         gown[cells] = project(a, h)
 
@@ -237,7 +260,15 @@
         finish(c)
 
     for c in range(COUNT):
-        for d in range(3):
+        if c in DETOUR:
+            @pl.when(p < n_pipe - 1)
+            def _():
+                share(c, 0).wait_send()
+
+            @pl.when(p == n_pipe - 1)
+            def _():
+                detour(c).wait_send()
+        for d in range(1 if c in DETOUR else 0, 3):
             share(c, d).wait_send()
 
         @pl.when(p < n_pipe - 1)
@@ -255,6 +286,14 @@
             def _():
                 keep_next(c).wait_send()
                 keep_next(c).wait_recv()
+
+    @pl.when(p == n_pipe - 2)
+    def _():
+        for c in DETOUR:
+            detour(c).wait_recv()
+            rejoin(c).start()
+        for c in DETOUR:
+            rejoin(c).wait_send()
 
 
 def solution(mesh):
@@ -283,9 +322,11 @@
                 pltpu.VMEM((3, cells, cut), BF16),
                 pltpu.VMEM((2, rows, half_cols, cut), BF16),
                 pltpu.VMEM((1, half_cols, width), BF16),
+                pltpu.VMEM((cells, cut), BF16),
                 dma((2,)), dma((2,)),
                 dma((3, COUNT)), dma((3, COUNT)),
                 dma((1,)), dma((1,)), dma((1,)), dma((2,)),
+                dma((COUNT,)), dma((COUNT,)), dma((COUNT,)),
                 dma((3, COUNT)), dma((3, COUNT)),
                 dma((COUNT,)), dma((COUNT,)),
                 dma((COUNT,)), dma((COUNT,)),

time: 110 us -> 110 us (level)
  no operation moved by 1% of the time
where the time goes in v6:
time: 110 us; the launch traced here: 109 us
  Pallas kernels  108 us (98%)
  local copies, waits for them, and re-layouts  1.67 us (2%)
    pallas_call x1, Pallas kernels, per_device(): pl.pallas_call(functools.partial(kernel, sizes), out_shape=jax.ShapeDtype...  108 us

profile of v6, /device:TPU:48, one launch (start us, length us, event | category | flops | bytes accessed | tf_op | source)
XLA Modules:
  0.0 109.4 jit_solution(17123290209976472974)
XLA Ops:
  0.0 107.7 %shard_map.46 = bf16[1,8,32,512]{3,2,1,0:T(8,128)(2,1)} custom-call(bf16[2,32,2048]{2,1,0:T(8,128)(2,1)} %stream.1, f32[1,2048]{1,0:T(1,128)} %scale.1, bf16[1,2048,512]{2,1,0:T(8,128)(2,1)} %wv_hbm.1, bf16[1,512,2048]{2,1,0:T(8,128)(2,1)} %wo_hbm.1), custom_call_target="tpu_custom_call" | custom-call | tf_op jit(solution)/shard_map/pallas_call | solution.py:308
  107.8 1.7 %copy.6 = bf16[1,8,32,512]{3,2,1,0:T(8,128)(2,1)} copy(bf16[1,8,32,512]{3,2,1,0:T(8,128)(2,1)} %shard_map.46) | data formatting | bytes 524288
